TPU v7x, 32 devices: a whole 2x2x4 slice. The times are simulated.
32 devices in a mesh: grp: 2 (over x), seq: 16 (over z, y, core).
Axes of the slice: x: 2, y: 2, z: 4, core: 2. Of those that a mesh axis runs over, the one named last changes fastest.
Arguments:
- queries: bfloat16 [6144, 4096], P(('grp', 'seq')), parts along dimension 0, may hold values from -6 to 6
- keys: bfloat16 [6144, 4096], P(('grp', 'seq')), parts along dimension 0, may hold values from -6 to 6
- values: bfloat16 [6144, 4096], P(('grp', 'seq')), parts along dimension 0, may hold values from -6 to 6
- latent_in: float32 [6144, 64], P(('grp', 'seq')), parts along dimension 0, may hold values from -6 to 6
- mod_table: float32 [16, 2, 4096], replicated, may hold values from -3 to 3
- step_size: float32 [16], replicated, may hold values from 0.25 to 1
- timestep: int32 [64], P('grp'), parts along dimension 0, may hold values from 0 to 15
- head_weight: float32 [4096, 64], replicated, may hold values from -0.09375 to 0.09375
- conv_in_weight: bfloat16 [27, 16, 384], replicated, may hold values from -0.3125 to 0.3125
- conv_in_bias: float32 [384], replicated, may hold values from -3 to 3
- norm_gain: float32 [384], replicated, may hold values from 0.1 to 1.9
- conv_weight: bfloat16 [27, 384, 384], replicated, may hold values from -0.0625 to 0.0625
- conv_bias: float32 [384], replicated, may hold values from -3 to 3
- patch_weight: bfloat16 [1536, 1024], replicated, may hold values from -0.15625 to 0.15625
- patch_gain: float32 [1024], replicated, may hold values from 0.1 to 1.9
- post_gain: float32 [1024], replicated, may hold values from 0.1 to 1.9
- proj_weight: float32 [1024, 768], replicated, may hold values from -0.1875 to 0.1875
- text_table: bfloat16 [24704, 768], P(None, 'seq'), may hold values from -6 to 6
- prompt_ids: int32 [154], P('grp'), parts along dimension 0, may hold values from 0 to 24703
- frame_order: int32 [64], P('grp'), parts along dimension 0, may hold values from 0 to 31, each once
Outputs:
- latent_next: float32 [6144, 64], P(('grp', 'seq')), parts along dimension 0
- decoded: bfloat16 [64, 16, 24, 384], P(('grp', 'seq')), parts along dimension 0
- image_embed: float32 [64, 768], P(('grp', 'seq')), parts along dimension 0
- scores: float32 [64], P(('grp', 'seq')), parts along dimension 0
There are 2 independent parts, one for each index of `grp`. A program takes and returns all parts, laid end to end along the dimension named above; an argument that names none is the same for every part. Nothing has to cross between parts.
All inputs are finite; a program needn't handle non-finite values.
Results may differ from a plain program's by a relative error of at most 0.009.
Values may be sent and summed in bfloat16 or wider, within the bound.
A program may use at most 128 MiB of HBM per device.

v0:
```python
import functools

import jax
import jax.numpy as jnp
from jax import lax
from jax.experimental import pallas as pl
from jax.experimental.pallas import tpu as pltpu
from jax.sharding import PartitionSpec as P

GRID_H = 8
GRID_W = 12
HEADS = 32
HD = 128
LAT_C = 16
CH = 384
TEXT_W = 768


highest = lax.Precision.HIGHEST


MESH = pl.DeviceIdType.MESH


def remote(src, dst, send, recv, device):
    return pltpu.make_async_remote_copy(
        src_ref=src, dst_ref=dst, send_sem=send, recv_sem=recv, device_id={"seq": device}, device_id_type=MESH
    )


def mix_kernel(
    n,
    heads_here,
    q_hbm,
    k_hbm,
    v_hbm,
    latent_ref,
    mod_hbm,
    step_ref,
    time_ref,
    weight_hbm,
    table_hbm,
    prompt_ref,
    latent_out,
    frames_out,
    text_out,
    k_buf,
    v_buf,
    q_buf,
    att_buf,
    part_buf,
    own_buf,
    mirror_buf,
    cross_buf,
    sum_buf,
    mod_buf,
    weight_buf,
    gain_buf,
    shift_buf,
    sum_rows,
    logit_even,
    logit_odd,
    peak_buf,
    halo_buf,
    table_buf,
    text_buf,
    text_all,
    k_send,
    k_recv,
    v_send,
    v_recv,
    q_send,
    q_recv,
    part_send,
    part_recv,
    cross_send,
    cross_recv,
    halo_send,
    halo_recv,
    text_send,
    text_recv,
    local_sem,
):
    me = lax.axis_index("seq")
    half = n // 2
    rows = q_buf.shape[1]
    wide = heads_here * HD
    cols_n = latent_ref.shape[0]
    frames_dev = rows // (GRID_H * GRID_W)
    per_frame = rows // frames_dev
    first_col = pl.multiple_of(me * wide, wide)

    locals_ = [pltpu.make_async_copy(mod_hbm, mod_buf, local_sem.at[0])]
    locals_.append(pltpu.make_async_copy(weight_hbm, weight_buf, local_sem.at[1]))
    own_cp = []
    for h in range(heads_here):
        own_col = pl.ds(pl.multiple_of(me * wide + h * HD, HD), HD)
        own_cp.append(pltpu.make_async_copy(k_hbm.at[:, own_col], k_buf.at[h, me], k_recv.at[h, me]))
        own_cp.append(pltpu.make_async_copy(v_hbm.at[:, own_col], v_buf.at[h, me, :, pl.ds(0, HD)], v_recv.at[h, me]))
    own_cp.append(pltpu.make_async_copy(q_hbm.at[:, pl.ds(first_col, wide)], q_buf.at[me], q_recv.at[me]))

    barrier = pltpu.get_barrier_semaphore()

    def greet(x, carry):
        pl.semaphore_signal(barrier, inc=1, device_id={"seq": jnp.bitwise_xor(me, x)}, device_id_type=MESH)
        return carry

    lax.fori_loop(1, n, greet, 0)
    pl.semaphore_wait(barrier, n - 1)

    def head_copy(hbm, buf, send, recv, h, peer):
        cols = pl.ds(pl.multiple_of(peer * wide + h * HD, HD), HD)
        return remote(
            hbm.at[:, cols], buf.at[h, me, :, pl.ds(0, HD)], send.at[h, peer], recv.at[h, me], peer
        )

    def query_copy(peer):
        cols = pl.ds(pl.multiple_of(peer * wide, wide), wide)
        return remote(q_hbm.at[:, cols], q_buf.at[me], q_send.at[peer], q_recv.at[me], peer)

    def send_some(make, first, last):
        def body(x, carry):
            make(jnp.bitwise_xor(me, x)).start()
            return carry

        lax.fori_loop(first, last, body, 0)

    def send_heads(h, first, last):
        send_some(lambda peer: head_copy(k_hbm, k_buf, k_send, k_recv, h, peer), first, last)
        send_some(lambda peer: head_copy(v_hbm, v_buf, v_send, v_recv, h, peer), first, last)

    beside_cut = jnp.logical_and(me >= half // 2, me < half + half // 2)
    send_heads(0, 1, half)
    send_some(query_copy, 1, half)
    for h in range(1, heads_here):
        send_heads(h, 1, half)
    for h in range(heads_here):
        send_heads(h, half, n)

    @pl.when(jnp.logical_not(beside_cut))
    def _():
        send_some(query_copy, half, n)

    for cp in locals_ + own_cp:
        cp.start()
    for cp in locals_:
        cp.wait()

    lanes = table_buf.shape[2]

    def table_part(i, carry):
        part = table_hbm.at[:, pl.ds(pl.multiple_of(i * lanes, lanes), lanes)]
        pltpu.make_async_copy(part, table_buf.at[i], local_sem.at[2]).start()
        return carry

    lax.fori_loop(0, table_buf.shape[0], table_part, 0)

    weight_own = weight_buf[:, pl.ds(first_col, wide)]

    def prepare(f, carry):
        gain = mod_buf[pl.ds(time_ref[f], 1), 1, pl.ds(first_col, wide)]
        scaled = (1.0 + gain) * weight_own
        high = scaled.astype(jnp.bfloat16)
        low = (scaled - high.astype(jnp.float32)).astype(jnp.bfloat16)
        gain_buf[f] = jnp.concatenate([high, low], axis=0)
        return carry

    lax.fori_loop(0, n * frames_dev, prepare, 0)

    def fill_ones(src, carry):
        for h in range(heads_here):
            v_buf[h, src, :, HD:] = jnp.ones((rows, HD), jnp.bfloat16)
        return carry

    lax.fori_loop(0, n, fill_ones, 0)

    def one_shift(head, carry):
        cols = pl.ds(pl.multiple_of(head * HD, HD), HD)
        shifts = jnp.concatenate(
            [mod_buf[pl.ds(time_ref[me * frames_dev + f], 1), 0, cols] for f in range(frames_dev)] * (8 // frames_dev),
            axis=0,
        )
        return carry + lax.dot_general(
            shifts,
            weight_buf[:, cols],
            (((1,), (1,)), ((), ())),
            precision=highest,
            preferred_element_type=jnp.float32,
        )

    shift_buf[...] = lax.fori_loop(0, HEADS, one_shift, jnp.zeros(shift_buf.shape, jnp.float32))

    words = prompt_ref.shape[0]
    width = table_buf.shape[1]
    lane_ids = lax.broadcasted_iota(jnp.int32, (width, lanes), 1)
    pltpu.make_async_copy(table_buf, table_buf, local_sem.at[2]).wait()

    def one_word(w, carry):
        word = prompt_ref[w]
        block = table_buf[word // lanes]
        return carry + jnp.where(lane_ids == word % lanes, block.astype(jnp.float32), 0.0)

    picked = lax.fori_loop(0, words, one_word, jnp.zeros((width, lanes), jnp.float32))
    text_buf[...] = jnp.broadcast_to(jnp.sum(picked, axis=-1, keepdims=True) / words, (width, lanes))

    def text_copy(peer):
        return remote(text_buf, text_all.at[me], text_send.at[peer], text_recv.at[me], peer)

    send_some(text_copy, 1, n)
    text_all[me] = text_buf[...]

    def arrived(buf, recv):
        def body(x, carry):
            block = buf.at[x, :, pl.ds(0, HD)]
            pltpu.make_async_copy(block, block, recv.at[x]).wait()
            return carry

        lax.fori_loop(0, n, body, 0)

    logit_bufs = (logit_even, logit_odd)

    def score(slot, h, src):
        logits = lax.dot_general(
            q_buf[src, :, h * HD : (h + 1) * HD],
            k_buf[h].reshape(n * rows, HD),
            (((1,), (1,)), ((), ())),
            preferred_element_type=jnp.float32,
        )
        logit_bufs[slot][...] = logits
        peak_buf[slot] = jnp.broadcast_to(jnp.max(logits, axis=-1, keepdims=True), (rows, HD))

    def weigh(slot, h, src):
        row_peak = peak_buf[slot, :, 0:1]
        exponent = jnp.exp2((logit_bufs[slot][...] - row_peak) * (HD ** (-0.5) * 1.4426950408889634))
        mixed = jnp.dot(
            exponent.astype(jnp.bfloat16),
            v_buf[h].reshape(n * rows, 2 * HD),
            preferred_element_type=jnp.float32,
        )
        att_buf[src, :, h * HD : (h + 1) * HD] = (mixed[:, :HD] / mixed[:, HD:]).astype(jnp.bfloat16)

    def in_turn(first, heads, waits, done):
        count = half * len(heads)
        unroll = 2 if len(heads) == 1 else len(heads)

        def place(t):
            x = first + lax.rem(t // len(heads), half)
            return x, jnp.bitwise_xor(me, x)

        def begin(t, p, guard):
            x, src = place(t)
            h = heads[p % len(heads)]
            if waits and p % len(heads) == 0:

                @pl.when(guard)
                def _():
                    pltpu.make_async_copy(q_buf.at[src], q_buf.at[src], q_recv.at[src]).wait()

            score(p % 2, h, src)

        begin(0, 0, me >= 0)

        def body(i, carry):
            for p in range(unroll):
                t = i * unroll + p
                begin(t + 1, p + 1, t + 1 < count)
                x, src = place(t)
                weigh(p % 2, heads[p % len(heads)], src)
                if p % len(heads) == len(heads) - 1:
                    done(x, src)
            return carry

        lax.fori_loop(0, count // unroll, body, 0)

    lane = lax.broadcasted_iota(jnp.int32, (per_frame, frames_dev * cols_n), 1)
    ones = jnp.ones((8, wide), jnp.bfloat16)
    turned = (((1,), (1,)), ((), ()))

    def project(x, src):
        packed = None
        for f in range(frames_dev):
            rows_a = att_buf[src, f * per_frame : (f + 1) * per_frame, :]
            both = lax.dot_general(
                rows_a, gain_buf[src * frames_dev + f], turned, preferred_element_type=jnp.float32
            )
            both = both + pltpu.roll(both, cols_n, 1)
            packed = both if packed is None else jnp.where(lane < f * cols_n, packed, both)
            rows_f = rows_a.astype(jnp.float32)
            squares = lax.dot_general(
                ones, (rows_f * rows_f).astype(jnp.bfloat16), turned, preferred_element_type=jnp.float32
            )
            sum_rows[x % 2, f * 8 : (f + 1) * 8, :per_frame] = squares
        part_buf[x, :per_frame, :] = packed.astype(jnp.bfloat16)
        part_buf[x, per_frame:, :] = sum_rows[x % 2].astype(jnp.bfloat16)

    for h in range(heads_here):
        arrived(k_buf.at[h], k_recv.at[h])
        arrived(v_buf.at[h], v_recv.at[h])
        if h == heads_here - 1:

            @pl.when(beside_cut)
            def _():
                send_some(query_copy, half, n)

        def near_done(x, src, h=h):
            if h == heads_here - 1:
                project(x, src)

                @pl.when(x > 0)
                def _():
                    remote(part_buf.at[x], own_buf.at[x], part_send.at[x], part_recv.at[x], src).start()

        in_turn(0, [h], h == 0, near_done)

    def far_done(x, src):
        project(x, src)

        @pl.when(x > half)
        def _():
            y = x - half
            to = jnp.bitwise_xor(me, y)
            remote(part_buf.at[x], mirror_buf.at[y], part_send.at[x], part_recv.at[x], to).start()

    in_turn(half, list(range(heads_here)), True, far_done)

    def part_wait(x):
        pltpu.make_async_copy(part_buf.at[x], part_buf.at[x], part_recv.at[x]).wait()

    total = part_buf[half].astype(jnp.float32)
    for y in range(1, half):
        part_wait(half + y)
        total = total + mirror_buf[y].astype(jnp.float32)
    sum_buf[...] = total.astype(jnp.bfloat16)
    cross = remote(sum_buf, cross_buf, cross_send, cross_recv, jnp.bitwise_xor(me, half))
    cross.start()
    total = part_buf[0].astype(jnp.float32)
    for y in range(1, half):
        part_wait(y)
        total = total + own_buf[y].astype(jnp.float32)
    cross.wait()
    total = total + cross_buf[...].astype(jnp.float32)
    diagonal = lax.broadcasted_iota(jnp.int32, (per_frame, per_frame), 0) == lax.broadcasted_iota(
        jnp.int32, (per_frame, per_frame), 1
    )
    latent_rows = jnp.transpose(latent_ref[...])
    pieces = []
    for f in range(frames_dev):
        row_sums = total[per_frame + f * 8 : per_frame + f * 8 + 1, :per_frame]
        meansq = jnp.sum(jnp.where(diagonal, row_sums, 0.0), axis=-1, keepdims=True) / (HEADS * HD)
        prediction = total[:per_frame, f * cols_n : (f + 1) * cols_n] * lax.rsqrt(meansq + 1e-06)
        moved = step_ref[time_ref[me * frames_dev + f]] * (prediction + shift_buf[f : f + 1, :])
        pieces.append(latent_rows[f * per_frame : (f + 1) * per_frame, :] + moved)
    latent_new = jnp.concatenate(pieces, axis=0)
    latent_wide = jnp.concatenate([latent_new, latent_new], axis=1)
    halo_buf[2] = latent_wide.astype(jnp.bfloat16)

    for back in (1, 2):
        step_to = remote(
            halo_buf.at[2], halo_buf.at[2 - back], halo_send.at[back - 1], halo_recv.at[back - 1], me + back
        )

        @pl.when(me + back < n)
        def _(step_to=step_to):
            step_to.start()

        @pl.when(me < back)
        def _(back=back):
            halo_buf[2 - back] = jnp.zeros(halo_buf.shape[1:], jnp.bfloat16)

    latent_out[...] = jnp.transpose(latent_new)

    def text_came(x, carry):
        src = jnp.bitwise_xor(me, x)
        pltpu.make_async_copy(text_all.at[src], text_all.at[src], text_recv.at[src]).wait()
        return carry

    lax.fori_loop(1, n, text_came, 0)
    text_out[...] = text_all[:, :, 0:8]

    for back in (1, 2):
        step_to = remote(
            halo_buf.at[2], halo_buf.at[2 - back], halo_send.at[back - 1], halo_recv.at[back - 1], me + back
        )

        @pl.when(me >= back)
        def _(step_to=step_to):
            step_to.wait_recv()

        @pl.when(me + back < n)
        def _(step_to=step_to):
            step_to.wait_send()

    frames_out[...] = halo_buf[...]

    def sent(x, carry):
        peer = jnp.bitwise_xor(me, x)
        for h in range(heads_here):
            head_copy(k_hbm, k_buf, k_send, k_recv, h, peer).wait_send()
            head_copy(v_hbm, v_buf, v_send, v_recv, h, peer).wait_send()
        query_copy(peer).wait_send()
        text_copy(peer).wait_send()
        return carry

    lax.fori_loop(1, n, sent, 0)

    def parts_sent(x, carry):
        remote(part_buf.at[x], own_buf.at[0], part_send.at[x], part_recv.at[x], jnp.bitwise_xor(me, 1)).wait_send()
        return carry

    lax.fori_loop(1, half, parts_sent, 0)
    lax.fori_loop(half + 1, n, parts_sent, 0)


def mix(queries, keys, values, latent_in, mod_table, step_size, timestep, head_weight, text_table, prompt_ids):
    n = lax.axis_size("seq")
    heads_here = HEADS // n
    rows, cols_n = latent_in.shape
    width = text_table.shape[1]
    wide = heads_here * HD
    half = n // 2
    frames_all = timestep.shape[0]
    frames_dev = frames_all // n
    part = (rows // frames_dev + 8 * frames_dev, frames_dev * cols_n)
    vmem = pltpu.VMEM
    dma = pltpu.SemaphoreType.DMA
    f32, b16 = jnp.float32, jnp.bfloat16
    anywhere = pl.BlockSpec(memory_space=pltpu.HBM)
    in_vmem = pl.BlockSpec(memory_space=pltpu.VMEM)
    in_smem = pl.BlockSpec(memory_space=pltpu.SMEM)
    return pl.pallas_call(
        functools.partial(mix_kernel, n, heads_here),
        out_shape=(
            jax.ShapeDtypeStruct((cols_n, rows), f32),
            jax.ShapeDtypeStruct((3, rows, 2 * cols_n), b16),
            jax.ShapeDtypeStruct((n, width, 8), f32),
        ),
        in_specs=[anywhere] * 3 + [in_vmem, anywhere, in_smem, in_smem, anywhere, anywhere, in_smem],
        out_specs=(in_vmem, in_vmem, in_vmem),
        scratch_shapes=[
            vmem((heads_here, n, rows, HD), b16),
            vmem((heads_here, n, rows, 2 * HD), b16),
            vmem((n, rows, wide), b16),
            vmem((n, rows, wide), b16),
            vmem((n,) + part, b16),
            vmem((half,) + part, b16),
            vmem((half,) + part, b16),
            vmem(part, b16),
            vmem(part, b16),
            vmem(mod_table.shape, f32),
            vmem((cols_n, HEADS * HD), f32),
            vmem((frames_all, 2 * cols_n, wide), b16),
            vmem((8, cols_n), f32),
            vmem((2, 8 * frames_dev, frames_dev * cols_n), f32),
            vmem((rows, n * rows), f32),
            vmem((rows, n * rows), f32),
            vmem((2, rows, HD), f32),
            vmem((3, rows, 2 * cols_n), b16),
            vmem((text_table.shape[0] // 128, width, 128), b16),
            vmem((width, 128), f32),
            vmem((n, width, 128), f32),
            dma((heads_here, n)),
            dma((heads_here, n)),
            dma((heads_here, n)),
            dma((heads_here, n)),
            dma((n,)),
            dma((n,)),
            dma((n,)),
            dma((n,)),
            dma,
            dma,
            dma((2,)),
            dma((2,)),
            dma((n,)),
            dma((n,)),
            dma((3,)),
        ],
        compiler_params=pltpu.CompilerParams(
            collective_id=0, has_side_effects=True, vmem_limit_bytes=67043328
        ),
        name="mix",
    )(
        queries,
        keys,
        values,
        latent_in.T,
        mod_table,
        step_size,
        timestep,
        head_weight.T,
        text_table.T,
        prompt_ids,
    )


TAPS = {(a, q): ((a + q - 1) % 2, (a + q - 1) // 2) for a in range(2) for q in range(3)}


def decode_kernel(
    n,
    halo_ref,
    text_ref,
    first_hbm,
    first_bias_ref,
    gain_ref,
    conv_hbm,
    conv_bias_ref,
    patch_hbm,
    patch_gain_ref,
    post_gain_ref,
    proj_hbm,
    order_ref,
    decoded_out,
    image_out,
    score_out,
    first_w,
    first_taps,
    wide_in,
    first_buf,
    window,
    conv_w,
    acc,
    pixels,
    patches,
    patch_w,
    proj_w,
    proj_pair,
    image_buf,
    image_all,
    image_send,
    image_recv,
    local_sem,
):
    me = lax.axis_index("seq")
    per_frame = GRID_H * GRID_W
    frames_dev = image_buf.shape[0]
    held = frames_dev + 2
    cols_n = halo_ref.shape[2] // 2
    lat_c = cols_n // 4
    ch = first_buf.shape[2]
    f32, b16 = jnp.float32, jnp.bfloat16

    copies = [
        pltpu.make_async_copy(src, dst, local_sem.at[i])
        for i, (src, dst) in enumerate(
            ((first_hbm, first_w), (conv_hbm, conv_w), (patch_hbm, patch_w), (proj_hbm, proj_w))
        )
    ]
    for cp in copies:
        cp.start()

    barrier = pltpu.get_barrier_semaphore()

    def greet(x, carry):
        pl.semaphore_signal(barrier, inc=1, device_id={"seq": jnp.bitwise_xor(me, x)}, device_id_type=MESH)
        return carry

    lax.fori_loop(1, n, greet, 0)

    latents = halo_ref[...].reshape(-1, 2 * cols_n).astype(f32)
    total_rows = latents.shape[0]
    token = lax.rem(lax.broadcasted_iota(jnp.int32, latents.shape, 0), per_frame)
    row_id, col_id = token // GRID_W, lax.rem(token, GRID_W)
    lane = lax.broadcasted_iota(jnp.int32, latents.shape, 1)
    for di in (-1, 0, 1):
        moved = []
        for dj in (-1, 0, 1):
            step = GRID_W * di + dj
            value = latents if step == 0 else pltpu.roll(latents, (-step) % total_rows, 0)
            keep = (row_id + di >= 0) & (row_id + di < GRID_H) & (col_id + dj >= 0) & (col_id + dj < GRID_W)
            moved.append(value if step == 0 else jnp.where(keep, value, 0.0))
        for b in range(2):
            pair = jnp.where(lane < cols_n, moved[b], moved[b + 1]).astype(b16)
            for a in range(2):
                u = di + 1 - a
                if 0 <= u < 2:
                    wide_in[2 * a + b, :, u * 2 * cols_n : (u + 1) * 2 * cols_n] = pair

    first_taps[...] = jnp.zeros_like(first_taps)
    copies[0].wait()
    for a in range(2):
        for b in range(2):
            for lag in range(3):
                for q in range(3):
                    for r in range(3):
                        (sub_a, di), (sub_b, dj) = TAPS[a, q], TAPS[b, r]
                        u, v = di + 1 - a, dj + 1 - b
                        at = ((u * 2 + v) * 4 + sub_a * 2 + sub_b) * lat_c
                        first_taps[2 * a + b, lag, at : at + lat_c, :] = first_w[lag * 9 + q * 3 + r]

    first_bias = first_bias_ref[...][None, :]
    for ab in range(4):
        summed = None
        for lag in range(3):
            term = jnp.dot(
                wide_in[ab, lag * per_frame : (lag + held) * per_frame, :],
                first_taps[ab, lag],
                preferred_element_type=f32,
            )
            summed = term if summed is None else summed + term
        first_buf[ab] = (summed + first_bias).astype(b16)

    gain = gain_ref[...][None, :]
    token = lax.broadcasted_iota(jnp.int32, (per_frame, ch), 0)
    row_id, col_id = token // GRID_W, lax.rem(token, GRID_W)

    def one_frame(f, carry):
        live = (me * frames_dev - 2 + f) >= 0
        span = pl.ds(pl.multiple_of(f * per_frame, per_frame), per_frame)
        for sub_a in range(2):
            for sub_b in range(2):
                first_f = first_buf[2 * sub_a + sub_b, span, :].astype(f32)
                meansq = jnp.mean(first_f * first_f, axis=-1, keepdims=True)
                value = jax.nn.silu(first_f * lax.rsqrt(meansq + 1e-06) * gain)
                value = jnp.where(live, value, 0.0)
                for di in (0, -1 if sub_a else 1):
                    for dj in (0, -1 if sub_b else 1):
                        step = GRID_W * di + dj
                        shifted = value
                        if step:
                            shifted = pltpu.roll(value, (-step) % per_frame, 0)
                            keep = (
                                (row_id + di >= 0)
                                & (row_id + di < GRID_H)
                                & (col_id + dj >= 0)
                                & (col_id + dj < GRID_W)
                            )
                            shifted = jnp.where(keep, shifted, 0.0)
                        shifted = shifted.astype(b16)
                        for (a, q), source_a in TAPS.items():
                            for (b, r), source_b in TAPS.items():
                                if source_a == (sub_a, di) and source_b == (sub_b, dj):
                                    tap = q * 3 + r
                                    window[f, 2 * a + b, :, tap * ch : (tap + 1) * ch] = shifted
        return carry

    lax.fori_loop(0, held, one_frame, 0)

    copies[1].wait()
    taps_n = 9
    conv_bias = conv_bias_ref[...][None, :]
    for f in range(frames_dev):
        for ab in range(4):
            own = first_buf[ab, (f + 2) * per_frame : (f + 3) * per_frame, :].astype(f32)
            acc[(f * 4 + ab) * per_frame : (f * 4 + ab + 1) * per_frame, :] = own + conv_bias

    def one_lag(lag, carry):
        rows = window[pl.ds(lag, frames_dev)].reshape(frames_dev * 4 * per_frame, taps_n * ch)
        weight = conv_w[pl.ds(lag * taps_n, taps_n)].reshape(taps_n * ch, ch)
        acc[...] += jnp.dot(rows, weight, preferred_element_type=f32)
        return carry

    lax.fori_loop(0, 3, one_lag, 0)

    for f in range(frames_dev):
        for a in range(2):
            for b in range(2):
                base = (f * 4 + 2 * a + b) * per_frame
                for i in range(GRID_H):
                    for c in range(pixels.shape[0]):
                        pixels[c, f, 2 * i + a, pl.ds(b, GRID_W, stride=2), :] = acc[
                            pl.ds(base + i * GRID_W, GRID_W), c * 128 : (c + 1) * 128
                        ]
                patches[f * per_frame : (f + 1) * per_frame, (2 * a + b) * ch : (2 * a + b + 1) * ch] = acc[
                    base : base + per_frame, :
                ].astype(b16)
    for c in range(pixels.shape[0]):
        decoded_out[:, :, :, c * 128 : (c + 1) * 128] = pixels[c].astype(b16)

    copies[2].wait()
    embedded = jnp.dot(patches[...], patch_w[...], preferred_element_type=f32).astype(b16).astype(f32)
    centered = embedded - jnp.mean(embedded, axis=-1, keepdims=True)
    variance = jnp.mean(centered * centered, axis=-1, keepdims=True)
    normed = centered * lax.rsqrt(variance + 1e-05)
    pooled = jnp.concatenate(
        [
            jnp.mean(normed[f * per_frame : (f + 1) * per_frame], axis=0, keepdims=True)
            for f in range(frames_dev)
        ],
        axis=0,
    ) * patch_gain_ref[...][None, :]
    centered = pooled - jnp.mean(pooled, axis=-1, keepdims=True)
    variance = jnp.mean(centered * centered, axis=-1, keepdims=True)
    pooled = centered * lax.rsqrt(variance + 1e-05) * post_gain_ref[...][None, :]

    copies[3].wait()
    pooled = jnp.concatenate([pooled] * (8 // frames_dev), axis=0)
    image = jnp.dot(pooled, proj_w[...], precision=highest, preferred_element_type=f32)
    for f in range(frames_dev):
        image_buf[f] = image[f : f + 1, :]

    pl.semaphore_wait(barrier, n - 1)

    def image_copy(peer):
        return remote(
            image_buf,
            image_all.at[pl.ds(me * frames_dev, frames_dev)],
            image_send.at[peer],
            image_recv.at[me],
            peer,
        )

    def spread(x, carry):
        image_copy(jnp.bitwise_xor(me, x)).start()
        return carry

    lax.fori_loop(1, n, spread, 0)
    image_all[pl.ds(me * frames_dev, frames_dev)] = image_buf[...]

    def came(x, carry):
        src = jnp.bitwise_xor(me, x)
        block = image_all.at[pl.ds(src * frames_dev, frames_dev)]
        pltpu.make_async_copy(block, block, image_recv.at[src]).wait()
        return carry

    lax.fori_loop(1, n, came, 0)
    text = text_ref[...]
    text_rms = jnp.sqrt(jnp.mean(text * text, keepdims=True) + 1e-06)
    for f in range(frames_dev):
        vector = image_all[order_ref[me * frames_dev + f]]
        image_out[f : f + 1, :] = vector
        inner = jnp.sum(vector * text, keepdims=True)
        image_rms = jnp.sqrt(jnp.mean(vector * vector, keepdims=True) + 1e-06)
        score_out[f] = (100.0 * inner / (TEXT_W * image_rms * text_rms))[0, 0]

    def gone(x, carry):
        image_copy(jnp.bitwise_xor(me, x)).wait_send()
        return carry

    lax.fori_loop(1, n, gone, 0)


def decode(
    halo,
    text_parts,
    conv_in_weight,
    conv_in_bias,
    norm_gain,
    conv_weight,
    conv_bias,
    patch_weight,
    patch_gain,
    post_gain,
    proj_weight,
    frame_order,
):
    n = lax.axis_size("seq")
    frames_dev = frame_order.shape[0] // n
    held = frames_dev + 2
    per_frame = GRID_H * GRID_W
    ch = conv_weight.shape[2]
    cols_n = halo.shape[2] // 2
    text_w = proj_weight.shape[1]
    vmem = pltpu.VMEM
    dma = pltpu.SemaphoreType.DMA
    f32, b16 = jnp.float32, jnp.bfloat16
    far = pl.BlockSpec(memory_space=pltpu.HBM)
    near = pl.BlockSpec(memory_space=pltpu.VMEM)
    scalars = pl.BlockSpec(memory_space=pltpu.SMEM)
    return pl.pallas_call(
        functools.partial(decode_kernel, n),
        out_shape=(
            jax.ShapeDtypeStruct((frames_dev, 2 * GRID_H, 2 * GRID_W, ch), b16),
            jax.ShapeDtypeStruct((frames_dev, text_w), f32),
            jax.ShapeDtypeStruct((frames_dev,), f32),
        ),
        in_specs=[near, near, far, near, near, far, near, far, near, near, far, scalars],
        out_specs=(near, near, scalars),
        scratch_shapes=[
            vmem(conv_in_weight.shape, b16),
            vmem((4, 3, 4 * cols_n, ch), b16),
            vmem((4, (held + 2) * per_frame, 4 * cols_n), b16),
            vmem((4, held * per_frame, ch), b16),
            vmem((held, 4, per_frame, 9 * ch), b16),
            vmem(conv_weight.shape, b16),
            vmem((frames_dev * 4 * per_frame, ch), f32),
            vmem((ch // 128, frames_dev, 2 * GRID_H, 2 * GRID_W, 128), f32),
            vmem((frames_dev * per_frame, 4 * ch), b16),
            vmem(patch_weight.shape, b16),
            vmem(proj_weight.shape, f32),
            vmem((8, 128), b16),
            vmem((frames_dev, 1, text_w), f32),
            vmem((n * frames_dev, 1, text_w), f32),
            dma((n,)),
            dma((n,)),
            dma((4,)),
        ],
        compiler_params=pltpu.CompilerParams(
            collective_id=1, has_side_effects=True, vmem_limit_bytes=67043328
        ),
        name="decode",
    )(
        halo,
        text_parts[:, :, 0].reshape(1, text_w),
        conv_in_weight,
        conv_in_bias,
        norm_gain,
        conv_weight,
        conv_bias,
        patch_weight,
        patch_gain,
        post_gain,
        proj_weight,
        frame_order,
    )


def local(
    queries,
    keys,
    values,
    latent_in,
    mod_table,
    step_size,
    timestep,
    head_weight,
    conv_in_weight,
    conv_in_bias,
    norm_gain,
    conv_weight,
    conv_bias,
    patch_weight,
    patch_gain,
    post_gain,
    proj_weight,
    text_table,
    prompt_ids,
    frame_order,
):
    latent_turned, halo, text_parts = mix(
        queries,
        keys,
        values,
        latent_in,
        mod_table,
        step_size,
        timestep,
        head_weight,
        text_table,
        prompt_ids,
    )
    decoded, image_vec, scores = decode(
        halo,
        text_parts,
        conv_in_weight,
        conv_in_bias,
        norm_gain,
        conv_weight,
        conv_bias,
        patch_weight,
        patch_gain,
        post_gain,
        proj_weight,
        frame_order,
    )
    return (latent_turned.T, decoded, image_vec, scores)


def solution(mesh):
    in_specs = (
        P(("grp", "seq"), None),
        P(("grp", "seq"), None),
        P(("grp", "seq"), None),
        P(("grp", "seq"), None),
        P(),
        P(),
        P("grp"),
        P(),
        P(),
        P(),
        P(),
        P(),
        P(),
        P(),
        P(),
        P(),
        P(),
        P(None, "seq"),
        P("grp"),
        P("grp"),
    )
    out_specs = (
        P(("grp", "seq"), None),
        P(("grp", "seq"), None, None, None),
        P(("grp", "seq"), None),
        P(("grp", "seq")),
    )
    return jax.shard_map(local, mesh=mesh, in_specs=in_specs, out_specs=out_specs, check_vma=False)
```

profile of v0, /device:TPU:0, one launch (start us, length us, event | category | flops | bytes accessed | tf_op | source)
XLA Modules:
  0.0 169.9 jit_solution(7866921824019294715)
XLA Ops:
  0.6 134.7 %mix.1 = (f32[64,192]{1,0:T(8,128)}, bf16[3,192,128]{2,1,0:T(8,128)(2,1)}, f32[16,48,8]{2,1,0:T(8,128)}) custom-call(bf16[192,4096]{1,0:T(8,128)(2,1)} %q_hbm.1, bf16[192,4096]{1,0:T(8,128)(2,1)} %k_hbm.1, bf16[192,4096]{1,0:T(8,128)(2,1)} %v_hbm.1, f32[64,192]{1,0:T(8,128)} %bitcast.6, f32[16,2,4096]{2,1,0:T(2,128)} %mod_hbm.1, f32[16]{0:T(128)} %step_ref.1, ...), custom_call_target="tpu_custom_call" | custom-call | tf_op jit(solution)/shard_map/mix/pallas_call | solution.py:430
  135.4 1.2 slice_reduce_fusion
  136.5 0.7 reshape_squeeze.3.text_ref
  137.2 26.8 %decode.1 = (bf16[2,16,24,384]{3,2,1,0:T(8,128)(2,1)}, f32[2,768]{1,0:T(2,128)}, f32[2]{0:T(128)}) custom-call(bf16[3,192,128]{2,1,0:T(8,128)(2,1)} %get-tuple-element.11.halo_ref, f32[1,768]{1,0:T(1,128)} %reshape_squeeze.3.text_ref, bf16[27,16,384]{2,1,0:T(8,128)(2,1)} %first_hbm.1, f32[384]{0:T(512)} %first_bias_ref.1, f32[384]{0:T(512)} %gain_ref.1, ...), custom_call_target="tpu_custom_call" | custom-call | tf_op jit(solution)/shard_map/decode/pallas_call | solution.py:759
  164.0 1.5 copy.28
  165.5 1.9 %copy.29 = bf16[2,16,24,384]{3,2,1,0:T(8,128)(2,1)} copy(bf16[2,16,24,384]{3,2,1,0:T(8,128)(2,1)} %get-tuple-element.21) | data formatting | bytes 1179648
  167.4 1.3 copy.30
  168.7 1.1 copy.31
where the time goes:
time: 170 us
  Pallas kernels  162 us (95%)
  local copies, waits for them, and re-layouts  7.66 us (5%)
    pallas_call x1, Pallas kernels, mix(): pl.pallas_call(functools.partial(mix_kernel, n, heads_here), out_shape=(j...  135 us
    pallas_call x1, Pallas kernels, decode(): pl.pallas_call(functools.partial(decode_kernel, n), out_shape=(jax.ShapeD...  26.8 us
    unnamed x4, local copies, waits for them, and re-layouts  5.82 us

commit v1 on v0

--- a/solution.py
+++ b/solution.py
@@ -41,8 +41,9 @@
     weight_hbm,
     table_hbm,
     prompt_ref,
+    early,
+    idle,
     latent_out,
-    frames_out,
     text_out,
     k_buf,
     v_buf,
@@ -129,20 +130,15 @@
         send_some(lambda peer: head_copy(k_hbm, k_buf, k_send, k_recv, h, peer), first, last)
         send_some(lambda peer: head_copy(v_hbm, v_buf, v_send, v_recv, h, peer), first, last)
 
-    beside_cut = jnp.logical_and(me >= half // 2, me < half + half // 2)
-    send_heads(0, 1, half)
+
+    send_heads(0, 1, n)
     send_some(query_copy, 1, half)
     for h in range(1, heads_here):
-        send_heads(h, 1, half)
-    for h in range(heads_here):
-        send_heads(h, half, n)
-
-    @pl.when(jnp.logical_not(beside_cut))
-    def _():
-        send_some(query_copy, half, n)
-
+        send_heads(h, 1, n)
+    send_some(query_copy, half, n)
     for cp in locals_ + own_cp:
         cp.start()
+    early()
     for cp in locals_:
         cp.wait()
 
@@ -201,13 +197,19 @@
         return carry + jnp.where(lane_ids == word % lanes, block.astype(jnp.float32), 0.0)
 
     picked = lax.fori_loop(0, words, one_word, jnp.zeros((width, lanes), jnp.float32))
-    text_buf[...] = jnp.broadcast_to(jnp.sum(picked, axis=-1, keepdims=True) / words, (width, lanes))
+    own_text = jnp.sum(picked, axis=-1, keepdims=True) / words
+    place = (width, n * width)
+    own_place = lax.broadcasted_iota(jnp.int32, place, 1) - me * width == lax.broadcasted_iota(
+        jnp.int32, place, 0
+    )
+    text_buf[...] = jnp.sum(jnp.where(own_place, own_text, 0.0), axis=0, keepdims=True)
 
     def text_copy(peer):
         return remote(text_buf, text_all.at[me], text_send.at[peer], text_recv.at[me], peer)
 
     send_some(text_copy, 1, n)
     text_all[me] = text_buf[...]
+    idle()
 
     def arrived(buf, recv):
         def body(x, carry):
@@ -296,12 +298,6 @@
     for h in range(heads_here):
         arrived(k_buf.at[h], k_recv.at[h])
         arrived(v_buf.at[h], v_recv.at[h])
-        if h == heads_here - 1:
-
-            @pl.when(beside_cut)
-            def _():
-                send_some(query_copy, half, n)
-
         def near_done(x, src, h=h):
             if h == heads_here - 1:
                 project(x, src)
@@ -375,7 +371,7 @@
         return carry
 
     lax.fori_loop(1, n, text_came, 0)
-    text_out[...] = text_all[:, :, 0:8]
+    text_out[...] = functools.reduce(jnp.add, [text_all[x] for x in range(n)])
 
     for back in (1, 2):
         step_to = remote(
@@ -390,106 +386,27 @@
         def _(step_to=step_to):
             step_to.wait_send()
 
-    frames_out[...] = halo_buf[...]
-
-    def sent(x, carry):
-        peer = jnp.bitwise_xor(me, x)
-        for h in range(heads_here):
-            head_copy(k_hbm, k_buf, k_send, k_recv, h, peer).wait_send()
-            head_copy(v_hbm, v_buf, v_send, v_recv, h, peer).wait_send()
-        query_copy(peer).wait_send()
-        text_copy(peer).wait_send()
-        return carry
-
-    lax.fori_loop(1, n, sent, 0)
-
-    def parts_sent(x, carry):
-        remote(part_buf.at[x], own_buf.at[0], part_send.at[x], part_recv.at[x], jnp.bitwise_xor(me, 1)).wait_send()
-        return carry
-
-    lax.fori_loop(1, half, parts_sent, 0)
-    lax.fori_loop(half + 1, n, parts_sent, 0)
-
-
-def mix(queries, keys, values, latent_in, mod_table, step_size, timestep, head_weight, text_table, prompt_ids):
-    n = lax.axis_size("seq")
-    heads_here = HEADS // n
-    rows, cols_n = latent_in.shape
-    width = text_table.shape[1]
-    wide = heads_here * HD
-    half = n // 2
-    frames_all = timestep.shape[0]
-    frames_dev = frames_all // n
-    part = (rows // frames_dev + 8 * frames_dev, frames_dev * cols_n)
-    vmem = pltpu.VMEM
-    dma = pltpu.SemaphoreType.DMA
-    f32, b16 = jnp.float32, jnp.bfloat16
-    anywhere = pl.BlockSpec(memory_space=pltpu.HBM)
-    in_vmem = pl.BlockSpec(memory_space=pltpu.VMEM)
-    in_smem = pl.BlockSpec(memory_space=pltpu.SMEM)
-    return pl.pallas_call(
-        functools.partial(mix_kernel, n, heads_here),
-        out_shape=(
-            jax.ShapeDtypeStruct((cols_n, rows), f32),
-            jax.ShapeDtypeStruct((3, rows, 2 * cols_n), b16),
-            jax.ShapeDtypeStruct((n, width, 8), f32),
-        ),
-        in_specs=[anywhere] * 3 + [in_vmem, anywhere, in_smem, in_smem, anywhere, anywhere, in_smem],
-        out_specs=(in_vmem, in_vmem, in_vmem),
-        scratch_shapes=[
-            vmem((heads_here, n, rows, HD), b16),
-            vmem((heads_here, n, rows, 2 * HD), b16),
-            vmem((n, rows, wide), b16),
-            vmem((n, rows, wide), b16),
-            vmem((n,) + part, b16),
-            vmem((half,) + part, b16),
-            vmem((half,) + part, b16),
-            vmem(part, b16),
-            vmem(part, b16),
-            vmem(mod_table.shape, f32),
-            vmem((cols_n, HEADS * HD), f32),
-            vmem((frames_all, 2 * cols_n, wide), b16),
-            vmem((8, cols_n), f32),
-            vmem((2, 8 * frames_dev, frames_dev * cols_n), f32),
-            vmem((rows, n * rows), f32),
-            vmem((rows, n * rows), f32),
-            vmem((2, rows, HD), f32),
-            vmem((3, rows, 2 * cols_n), b16),
-            vmem((text_table.shape[0] // 128, width, 128), b16),
-            vmem((width, 128), f32),
-            vmem((n, width, 128), f32),
-            dma((heads_here, n)),
-            dma((heads_here, n)),
-            dma((heads_here, n)),
-            dma((heads_here, n)),
-            dma((n,)),
-            dma((n,)),
-            dma((n,)),
-            dma((n,)),
-            dma,
-            dma,
-            dma((2,)),
-            dma((2,)),
-            dma((n,)),
-            dma((n,)),
-            dma((3,)),
-        ],
-        compiler_params=pltpu.CompilerParams(
-            collective_id=0, has_side_effects=True, vmem_limit_bytes=67043328
-        ),
-        name="mix",
-    )(
-        queries,
-        keys,
-        values,
-        latent_in.T,
-        mod_table,
-        step_size,
-        timestep,
-        head_weight.T,
-        text_table.T,
-        prompt_ids,
-    )
+
+    def finish():
+        def sent(x, carry):
+            peer = jnp.bitwise_xor(me, x)
+            for h in range(heads_here):
+                head_copy(k_hbm, k_buf, k_send, k_recv, h, peer).wait_send()
+                head_copy(v_hbm, v_buf, v_send, v_recv, h, peer).wait_send()
+            query_copy(peer).wait_send()
+            text_copy(peer).wait_send()
+            return carry
+
+        lax.fori_loop(1, n, sent, 0)
+
+        def parts_sent(x, carry):
+            remote(part_buf.at[x], own_buf.at[0], part_send.at[x], part_recv.at[x], jnp.bitwise_xor(me, 1)).wait_send()
+            return carry
+
+        lax.fori_loop(1, half, parts_sent, 0)
+        lax.fori_loop(half + 1, n, parts_sent, 0)
+
+    return finish
 
 
 TAPS = {(a, q): ((a + q - 1) % 2, (a + q - 1) // 2) for a in range(2) for q in range(3)}
@@ -523,7 +440,7 @@
     patches,
     patch_w,
     proj_w,
-    proj_pair,
+    decoded_buf,
     image_buf,
     image_all,
     image_send,
@@ -539,22 +456,33 @@
     ch = first_buf.shape[2]
     f32, b16 = jnp.float32, jnp.bfloat16
 
+    out_copy = pltpu.make_async_copy(decoded_buf, decoded_out, local_sem.at[4])
     copies = [
         pltpu.make_async_copy(src, dst, local_sem.at[i])
         for i, (src, dst) in enumerate(
             ((first_hbm, first_w), (conv_hbm, conv_w), (patch_hbm, patch_w), (proj_hbm, proj_w))
         )
     ]
-    for cp in copies:
-        cp.start()
-
-    barrier = pltpu.get_barrier_semaphore()
-
-    def greet(x, carry):
-        pl.semaphore_signal(barrier, inc=1, device_id={"seq": jnp.bitwise_xor(me, x)}, device_id_type=MESH)
-        return carry
-
-    lax.fori_loop(1, n, greet, 0)
+    def early():
+        for cp in copies:
+            cp.start()
+
+    def idle():
+        first_taps[...] = jnp.zeros_like(first_taps)
+        copies[0].wait()
+        for a in range(2):
+            for b in range(2):
+                for lag in range(3):
+                    for q in range(3):
+                        for r in range(3):
+                            (sub_a, di), (sub_b, dj) = TAPS[a, q], TAPS[b, r]
+                            u, v = di + 1 - a, dj + 1 - b
+                            at = ((u * 2 + v) * 4 + sub_a * 2 + sub_b) * lat_c
+                            first_taps[2 * a + b, lag, at : at + lat_c, :] = first_w[lag * 9 + q * 3 + r]
+        for cp in copies[1:]:
+            cp.wait()
+
+    yield early, idle
 
     latents = halo_ref[...].reshape(-1, 2 * cols_n).astype(f32)
     total_rows = latents.shape[0]
@@ -574,18 +502,6 @@
                 u = di + 1 - a
                 if 0 <= u < 2:
                     wide_in[2 * a + b, :, u * 2 * cols_n : (u + 1) * 2 * cols_n] = pair
-
-    first_taps[...] = jnp.zeros_like(first_taps)
-    copies[0].wait()
-    for a in range(2):
-        for b in range(2):
-            for lag in range(3):
-                for q in range(3):
-                    for r in range(3):
-                        (sub_a, di), (sub_b, dj) = TAPS[a, q], TAPS[b, r]
-                        u, v = di + 1 - a, dj + 1 - b
-                        at = ((u * 2 + v) * 4 + sub_a * 2 + sub_b) * lat_c
-                        first_taps[2 * a + b, lag, at : at + lat_c, :] = first_w[lag * 9 + q * 3 + r]
 
     first_bias = first_bias_ref[...][None, :]
     for ab in range(4):
@@ -635,7 +551,6 @@
 
     lax.fori_loop(0, held, one_frame, 0)
 
-    copies[1].wait()
     taps_n = 9
     conv_bias = conv_bias_ref[...][None, :]
     for f in range(frames_dev):
@@ -664,9 +579,9 @@
                     base : base + per_frame, :
                 ].astype(b16)
     for c in range(pixels.shape[0]):
-        decoded_out[:, :, :, c * 128 : (c + 1) * 128] = pixels[c].astype(b16)
-
-    copies[2].wait()
+        decoded_buf[:, :, :, c * 128 : (c + 1) * 128] = pixels[c].astype(b16)
+    out_copy.start()
+
     embedded = jnp.dot(patches[...], patch_w[...], preferred_element_type=f32).astype(b16).astype(f32)
     centered = embedded - jnp.mean(embedded, axis=-1, keepdims=True)
     variance = jnp.mean(centered * centered, axis=-1, keepdims=True)
@@ -682,13 +597,10 @@
     variance = jnp.mean(centered * centered, axis=-1, keepdims=True)
     pooled = centered * lax.rsqrt(variance + 1e-05) * post_gain_ref[...][None, :]
 
-    copies[3].wait()
     pooled = jnp.concatenate([pooled] * (8 // frames_dev), axis=0)
     image = jnp.dot(pooled, proj_w[...], precision=highest, preferred_element_type=f32)
     for f in range(frames_dev):
         image_buf[f] = image[f : f + 1, :]
-
-    pl.semaphore_wait(barrier, n - 1)
 
     def image_copy(peer):
         return remote(
@@ -727,11 +639,37 @@
         return carry
 
     lax.fori_loop(1, n, gone, 0)
-
-
-def decode(
-    halo,
-    text_parts,
+    out_copy.wait()
+    yield
+
+
+MIX_IN, DECODE_IN, MIX_SCRATCH, HALO_AT = 10, 10, 36, 17
+
+
+def whole_kernel(n, heads_here, *refs):
+    mix_in, refs = refs[:MIX_IN], refs[MIX_IN:]
+    decode_in, refs = refs[:DECODE_IN], refs[DECODE_IN:]
+    (latent_out, decoded_out, image_out, score_out), refs = refs[:4], refs[4:]
+    (text_full, *mix_scratch), decode_scratch = refs[: MIX_SCRATCH + 1], refs[MIX_SCRATCH + 1 :]
+    halo_buf = mix_scratch[HALO_AT]
+    steps = decode_kernel(n, halo_buf, text_full, *decode_in, decoded_out, image_out, score_out, *decode_scratch)
+    early, idle = next(steps)
+    finish = mix_kernel(n, heads_here, *mix_in, early, idle, latent_out, text_full, *mix_scratch)
+    next(steps)
+    finish()
+
+
+def everything(
+    queries,
+    keys,
+    values,
+    latent_in,
+    mod_table,
+    step_size,
+    timestep,
+    head_weight,
+    text_table,
+    prompt_ids,
     conv_in_weight,
     conv_in_bias,
     norm_gain,
@@ -744,53 +682,111 @@
     frame_order,
 ):
     n = lax.axis_size("seq")
-    frames_dev = frame_order.shape[0] // n
+    heads_here = HEADS // n
+    rows, cols_n = latent_in.shape
+    width = text_table.shape[1]
+    wide = heads_here * HD
+    half = n // 2
+    frames_all = timestep.shape[0]
+    frames_dev = frames_all // n
+    per_frame = rows // frames_dev
+    part = (per_frame + 8 * frames_dev, frames_dev * cols_n)
     held = frames_dev + 2
-    per_frame = GRID_H * GRID_W
     ch = conv_weight.shape[2]
-    cols_n = halo.shape[2] // 2
     text_w = proj_weight.shape[1]
+    pixel_shape = (frames_dev, 2 * GRID_H, 2 * GRID_W, ch)
     vmem = pltpu.VMEM
     dma = pltpu.SemaphoreType.DMA
     f32, b16 = jnp.float32, jnp.bfloat16
     far = pl.BlockSpec(memory_space=pltpu.HBM)
     near = pl.BlockSpec(memory_space=pltpu.VMEM)
     scalars = pl.BlockSpec(memory_space=pltpu.SMEM)
-    return pl.pallas_call(
-        functools.partial(decode_kernel, n),
+    mix_scratch = [
+        vmem((heads_here, n, rows, HD), b16),
+        vmem((heads_here, n, rows, 2 * HD), b16),
+        vmem((n, rows, wide), b16),
+        vmem((n, rows, wide), b16),
+        vmem((n,) + part, b16),
+        vmem((half,) + part, b16),
+        vmem((half,) + part, b16),
+        vmem(part, b16),
+        vmem(part, b16),
+        vmem(mod_table.shape, f32),
+        vmem((cols_n, HEADS * HD), f32),
+        vmem((frames_all, 2 * cols_n, wide), b16),
+        vmem((8, cols_n), f32),
+        vmem((2, 8 * frames_dev, frames_dev * cols_n), f32),
+        vmem((rows, n * rows), f32),
+        vmem((rows, n * rows), f32),
+        vmem((2, rows, HD), f32),
+        vmem((3, rows, 2 * cols_n), b16),
+        vmem((text_table.shape[0] // 128, width, 128), b16),
+        vmem((1, n * width), f32),
+        vmem((n, 1, n * width), f32),
+        dma((heads_here, n)),
+        dma((heads_here, n)),
+        dma((heads_here, n)),
+        dma((heads_here, n)),
+        dma((n,)),
+        dma((n,)),
+        dma((n,)),
+        dma((n,)),
+        dma,
+        dma,
+        dma((2,)),
+        dma((2,)),
+        dma((n,)),
+        dma((n,)),
+        dma((3,)),
+    ]
+    decode_scratch = [
+        vmem(conv_in_weight.shape, b16),
+        vmem((4, 3, 4 * cols_n, ch), b16),
+        vmem((4, (held + 2) * per_frame, 4 * cols_n), b16),
+        vmem((4, held * per_frame, ch), b16),
+        vmem((held, 4, per_frame, 9 * ch), b16),
+        vmem(conv_weight.shape, b16),
+        vmem((frames_dev * 4 * per_frame, ch), f32),
+        vmem((ch // 128, frames_dev, 2 * GRID_H, 2 * GRID_W, 128), f32),
+        vmem((frames_dev * per_frame, 4 * ch), b16),
+        vmem(patch_weight.shape, b16),
+        vmem(proj_weight.shape, f32),
+        vmem(pixel_shape, b16),
+        vmem((frames_dev, 1, text_w), f32),
+        vmem((n * frames_dev, 1, text_w), f32),
+        dma((n,)),
+        dma((n,)),
+        dma((5,)),
+    ]
+    assert len(mix_scratch) == MIX_SCRATCH
+    results = pl.pallas_call(
+        functools.partial(whole_kernel, n, heads_here),
         out_shape=(
-            jax.ShapeDtypeStruct((frames_dev, 2 * GRID_H, 2 * GRID_W, ch), b16),
+            jax.ShapeDtypeStruct((cols_n, rows), f32),
+            jax.ShapeDtypeStruct(pixel_shape, b16),
             jax.ShapeDtypeStruct((frames_dev, text_w), f32),
             jax.ShapeDtypeStruct((frames_dev,), f32),
         ),
-        in_specs=[near, near, far, near, near, far, near, far, near, near, far, scalars],
-        out_specs=(near, near, scalars),
-        scratch_shapes=[
-            vmem(conv_in_weight.shape, b16),
-            vmem((4, 3, 4 * cols_n, ch), b16),
-            vmem((4, (held + 2) * per_frame, 4 * cols_n), b16),
-            vmem((4, held * per_frame, ch), b16),
-            vmem((held, 4, per_frame, 9 * ch), b16),
-            vmem(conv_weight.shape, b16),
-            vmem((frames_dev * 4 * per_frame, ch), f32),
-            vmem((ch // 128, frames_dev, 2 * GRID_H, 2 * GRID_W, 128), f32),
-            vmem((frames_dev * per_frame, 4 * ch), b16),
-            vmem(patch_weight.shape, b16),
-            vmem(proj_weight.shape, f32),
-            vmem((8, 128), b16),
-            vmem((frames_dev, 1, text_w), f32),
-            vmem((n * frames_dev, 1, text_w), f32),
-            dma((n,)),
-            dma((n,)),
-            dma((4,)),
-        ],
+        in_specs=[far] * 3
+        + [near, far, scalars, scalars, far, far, scalars]
+        + [far, near, near, far, near, far, near, near, far, scalars],
+        out_specs=(near, far, near, scalars),
+        scratch_shapes=[vmem((1, text_w), f32)] + mix_scratch + decode_scratch,
         compiler_params=pltpu.CompilerParams(
-            collective_id=1, has_side_effects=True, vmem_limit_bytes=67043328
+            collective_id=0, has_side_effects=True, vmem_limit_bytes=67043328
         ),
-        name="decode",
+        name="everything",
     )(
-        halo,
-        text_parts[:, :, 0].reshape(1, text_w),
+        queries,
+        keys,
+        values,
+        latent_in.T,
+        mod_table,
+        step_size,
+        timestep,
+        head_weight.T,
+        text_table.T,
+        prompt_ids,
         conv_in_weight,
         conv_in_bias,
         norm_gain,
@@ -802,6 +798,27 @@
         proj_weight,
         frame_order,
     )
+    return deliver(*results)
+
+
+def deliver_kernel(*refs):
+    count = len(refs) // 2
+    for source, target in zip(refs[: count - 1], refs[count:-1]):
+        target[...] = source[...]
+    for f in range(refs[-1].shape[0]):
+        refs[-1][f] = refs[count - 1][f]
+
+
+def deliver(*arrays):
+    near = pl.BlockSpec(memory_space=pltpu.VMEM)
+    specs = [near] * (len(arrays) - 1) + [pl.BlockSpec(memory_space=pltpu.SMEM)]
+    return pl.pallas_call(
+        deliver_kernel,
+        out_shape=[jax.ShapeDtypeStruct(a.shape, a.dtype) for a in arrays],
+        in_specs=specs,
+        out_specs=specs,
+        name="deliver",
+    )(*arrays)
 
 
 def local(
@@ -826,7 +843,7 @@
     prompt_ids,
     frame_order,
 ):
-    latent_turned, halo, text_parts = mix(
+    latent_turned, decoded, image_vec, scores = everything(
         queries,
         keys,
         values,
@@ -837,10 +854,6 @@
         head_weight,
         text_table,
         prompt_ids,
-    )
-    decoded, image_vec, scores = decode(
-        halo,
-        text_parts,
         conv_in_weight,
         conv_in_bias,
         norm_gain,

time: 170 us -> 158 us (0.929)
  local copies, waits for them, and re-layouts: 7.66 us -> 0 us
  Pallas kernels: 162 us -> 157 us
    unnamed x4 -> x0, local copies, waits for them, and re-layouts: 5.82 us -> none
    pallas_call x2, Pallas kernels: 162 us -> 157 us  [the longest x1 155 us: everything(): pl.pallas_call(functools.partial(whole_kernel, n, heads_here), out_shape=...]
where the time goes in v1:
time: 158 us
  Pallas kernels  157 us (99%)
    pallas_call x1, Pallas kernels, everything(): pl.pallas_call(functools.partial(whole_kernel, n, heads_here), out_shape=...  155 us

profile of v1, /device:TPU:0, one launch (start us, length us, event | category | flops | bytes accessed | tf_op | source)
XLA Modules:
  0.0 157.7 jit_solution(6702181536929022487)
XLA Ops:
  0.6 154.9 %everything.1 = (f32[64,192]{1,0:T(8,128)}, bf16[2,16,24,384]{3,2,1,0:T(8,128)(2,1)}, f32[2,768]{1,0:T(2,128)}, f32[2]{0:T(128)}) custom-call(bf16[192,4096]{1,0:T(8,128)(2,1)} %refs_0_.1, bf16[192,4096]{1,0:T(8,128)(2,1)} %refs_1_.1, bf16[192,4096]{1,0:T(8,128)(2,1)} %refs_2_.1, f32[64,192]{1,0:T(8,128)} %bitcast.6, f32[16,2,4096]{2,1,0:T(2,128)} %refs_4_.1, ...), custom_call_target="tpu_custom_call" | custom-call | tf_op jit(solution)/shard_map/everything/pallas_call | solution.py:762
  155.5 2.0 %deliver.1 = (f32[64,192]{1,0:T(8,128)}, bf16[2,16,24,384]{3,2,1,0:T(8,128)(2,1)}, f32[2,768]{1,0:T(2,128)}, f32[2]{0:T(128)}) custom-call(f32[64,192]{1,0:T(8,128)} %get-tuple-element.12.refs_0_, bf16[2,16,24,384]{3,2,1,0:T(8,128)(2,1)} %get-tuple-element.13.refs_1_, f32[2,768]{1,0:T(2,128)} %get-tuple-element.14.refs_2_, f32[2]{0:T(128)} %get-tuple-element.15.refs_3_), custom_call_target="tpu_custom_call" | custom-call | tf_op jit(solution)/shard_map/deliver/pallas_call | solution.py:815

commit v2 on v1

--- a/solution.py
+++ b/solution.py
@@ -20,6 +20,7 @@
 
 
 MESH = pl.DeviceIdType.MESH
+AHEAD = 4
 
 
 def remote(src, dst, send, recv, device):
@@ -126,22 +127,44 @@
 
         lax.fori_loop(first, last, body, 0)
 
-    def send_heads(h, first, last):
-        send_some(lambda peer: head_copy(k_hbm, k_buf, k_send, k_recv, h, peer), first, last)
-        send_some(lambda peer: head_copy(v_hbm, v_buf, v_send, v_recv, h, peer), first, last)
-
-
-    send_heads(0, 1, n)
+    phases = []
+    for h in range(heads_here):
+        phases.append(lambda peer, h=h: head_copy(k_hbm, k_buf, k_send, k_recv, h, peer))
+        phases.append(lambda peer, h=h: head_copy(v_hbm, v_buf, v_send, v_recv, h, peer))
+
+    def follow(phase):
+        def body(x, carry):
+            peer = jnp.bitwise_xor(me, x)
+            phases[phase](peer).wait_send()
+            if phase + 1 < len(phases):
+                phases[phase + 1](peer).start()
+            else:
+
+                @pl.when(x < half + AHEAD)
+                def _():
+                    query_copy(peer).start()
+
+            return carry
+
+        lax.fori_loop(half, n, body, 0)
+
+    def follow_query(x):
+        query_copy(jnp.bitwise_xor(me, x)).wait_send()
+
+        @pl.when(x + AHEAD < n)
+        def _():
+            query_copy(jnp.bitwise_xor(me, x + AHEAD)).start()
+
+    send_some(phases[0], 1, n)
+    send_some(phases[1], 1, half)
     send_some(query_copy, 1, half)
-    for h in range(1, heads_here):
-        send_heads(h, 1, n)
-    send_some(query_copy, half, n)
     for cp in locals_ + own_cp:
         cp.start()
     early()
     for cp in locals_:
         cp.wait()
 
+    follow(0)
     lanes = table_buf.shape[2]
 
     def table_part(i, carry):
@@ -256,6 +279,8 @@
 
                 @pl.when(guard)
                 def _():
+                    if first > 0:
+                        follow_query(x)
                     pltpu.make_async_copy(q_buf.at[src], q_buf.at[src], q_recv.at[src]).wait()
 
             score(p % 2, h, src)
@@ -296,6 +321,12 @@
         part_buf[x, per_frame:, :] = sum_rows[x % 2].astype(jnp.bfloat16)
 
     for h in range(heads_here):
+        if h > 0:
+            follow(2 * h)
+        if h + 1 < heads_here:
+            send_some(phases[2 * h + 2], 1, half)
+            send_some(phases[2 * h + 3], 1, half)
+        follow(2 * h + 1)
         arrived(k_buf.at[h], k_recv.at[h])
         arrived(v_buf.at[h], v_recv.at[h])
         def near_done(x, src, h=h):
@@ -388,16 +419,17 @@
 
 
     def finish():
-        def sent(x, carry):
-            peer = jnp.bitwise_xor(me, x)
-            for h in range(heads_here):
-                head_copy(k_hbm, k_buf, k_send, k_recv, h, peer).wait_send()
-                head_copy(v_hbm, v_buf, v_send, v_recv, h, peer).wait_send()
-            query_copy(peer).wait_send()
-            text_copy(peer).wait_send()
+        def near_sent(x, carry):
+            for copy in phases + [query_copy]:
+                copy(jnp.bitwise_xor(me, x)).wait_send()
             return carry
 
-        lax.fori_loop(1, n, sent, 0)
+        def text_sent(x, carry):
+            text_copy(jnp.bitwise_xor(me, x)).wait_send()
+            return carry
+
+        lax.fori_loop(1, half, near_sent, 0)
+        lax.fori_loop(1, n, text_sent, 0)
 
         def parts_sent(x, carry):
             remote(part_buf.at[x], own_buf.at[0], part_send.at[x], part_recv.at[x], jnp.bitwise_xor(me, 1)).wait_send()
@@ -440,6 +472,8 @@
     patches,
     patch_w,
     proj_w,
+    proj_high,
+    proj_low,
     decoded_buf,
     image_buf,
     image_all,
@@ -481,6 +515,10 @@
                             first_taps[2 * a + b, lag, at : at + lat_c, :] = first_w[lag * 9 + q * 3 + r]
         for cp in copies[1:]:
             cp.wait()
+        whole = proj_w[...]
+        high = whole.astype(b16)
+        proj_high[...] = high
+        proj_low[...] = (whole - high.astype(f32)).astype(b16)
 
     yield early, idle
 
@@ -597,8 +635,12 @@
     variance = jnp.mean(centered * centered, axis=-1, keepdims=True)
     pooled = centered * lax.rsqrt(variance + 1e-05) * post_gain_ref[...][None, :]
 
-    pooled = jnp.concatenate([pooled] * (8 // frames_dev), axis=0)
-    image = jnp.dot(pooled, proj_w[...], precision=highest, preferred_element_type=f32)
+    pooled_high = pooled.astype(b16).astype(f32)
+    blank = jnp.zeros((16 - 2 * frames_dev, pooled.shape[1]), f32)
+    pair = jnp.concatenate([pooled_high, pooled - pooled_high, blank], axis=0).astype(b16)
+    main = jnp.dot(pair, proj_high[...], preferred_element_type=f32)
+    rest = jnp.dot(pair, proj_low[...], preferred_element_type=f32)
+    image = main[:frames_dev] + (main[frames_dev : 2 * frames_dev] + rest[:frames_dev])
     for f in range(frames_dev):
         image_buf[f] = image[f : f + 1, :]
 
@@ -644,6 +686,7 @@
 
 
 MIX_IN, DECODE_IN, MIX_SCRATCH, HALO_AT = 10, 10, 36, 17
+SMALL_MIX, SMALL_DECODE = (3, 5, 6, 9), (1, 2, 4, 6, 7, 9)
 
 
 def whole_kernel(n, heads_here, *refs):
@@ -652,8 +695,25 @@
     (latent_out, decoded_out, image_out, score_out), refs = refs[:4], refs[4:]
     (text_full, *mix_scratch), decode_scratch = refs[: MIX_SCRATCH + 1], refs[MIX_SCRATCH + 1 :]
     halo_buf = mix_scratch[HALO_AT]
+    *decode_scratch, small_sem = decode_scratch
+    small_bufs = decode_scratch[-len(SMALL_MIX) - len(SMALL_DECODE) :]
+    decode_scratch = decode_scratch[: -len(small_bufs)]
+    mix_in, decode_in = list(mix_in), list(decode_in)
+    small_copies = []
+    for group, places in ((mix_in, SMALL_MIX), (decode_in, SMALL_DECODE)):
+        for place in places:
+            i = len(small_copies)
+            small_copies.append(pltpu.make_async_copy(group[place], small_bufs[i], small_sem.at[i]))
+            small_copies[-1].start()
+            group[place] = small_bufs[i]
     steps = decode_kernel(n, halo_buf, text_full, *decode_in, decoded_out, image_out, score_out, *decode_scratch)
-    early, idle = next(steps)
+    start_weights, idle = next(steps)
+
+    def early():
+        start_weights()
+        for cp in small_copies:
+            cp.wait()
+
     finish = mix_kernel(n, heads_here, *mix_in, early, idle, latent_out, text_full, *mix_scratch)
     next(steps)
     finish()
@@ -751,12 +811,25 @@
         vmem((frames_dev * per_frame, 4 * ch), b16),
         vmem(patch_weight.shape, b16),
         vmem(proj_weight.shape, f32),
+        vmem(proj_weight.shape, b16),
+        vmem(proj_weight.shape, b16),
         vmem(pixel_shape, b16),
         vmem((frames_dev, 1, text_w), f32),
         vmem((n * frames_dev, 1, text_w), f32),
         dma((n,)),
         dma((n,)),
         dma((5,)),
+        vmem((cols_n, rows), f32),
+        pltpu.SMEM(step_size.shape, f32),
+        pltpu.SMEM(timestep.shape, jnp.int32),
+        pltpu.SMEM(prompt_ids.shape, jnp.int32),
+        vmem(conv_in_bias.shape, f32),
+        vmem(norm_gain.shape, f32),
+        vmem(conv_bias.shape, f32),
+        vmem(patch_gain.shape, f32),
+        vmem(post_gain.shape, f32),
+        pltpu.SMEM(frame_order.shape, jnp.int32),
+        dma((len(SMALL_MIX) + len(SMALL_DECODE),)),
     ]
     assert len(mix_scratch) == MIX_SCRATCH
     results = pl.pallas_call(
@@ -767,9 +840,7 @@
             jax.ShapeDtypeStruct((frames_dev, text_w), f32),
             jax.ShapeDtypeStruct((frames_dev,), f32),
         ),
-        in_specs=[far] * 3
-        + [near, far, scalars, scalars, far, far, scalars]
-        + [far, near, near, far, near, far, near, near, far, scalars],
+        in_specs=[far] * (MIX_IN + DECODE_IN),
         out_specs=(near, far, near, scalars),
         scratch_shapes=[vmem((1, text_w), f32)] + mix_scratch + decode_scratch,
         compiler_params=pltpu.CompilerParams(

time: 158 us -> 154 us (0.975)
  Pallas kernels: 157 us -> 153 us
    pallas_call x1, Pallas kernels: 155 us -> 151 us  [everything(): pl.pallas_call(functools.partial(whole_kernel, n, heads_here), out_shape=...]
where the time goes in v2:
time: 154 us
  Pallas kernels  153 us (99%)
    pallas_call x1, Pallas kernels, everything(): pl.pallas_call(functools.partial(whole_kernel, n, heads_here), out_shape=...  151 us

profile of v2, /device:TPU:0, one launch (start us, length us, event | category | flops | bytes accessed | tf_op | source)
XLA Modules:
  0.0 153.7 jit_solution(8943123379068988358)
XLA Ops:
  0.6 150.9 %everything.1 = (f32[64,192]{1,0:T(8,128)}, bf16[2,16,24,384]{3,2,1,0:T(8,128)(2,1)}, f32[2,768]{1,0:T(2,128)}, f32[2]{0:T(128)}) custom-call(bf16[192,4096]{1,0:T(8,128)(2,1)} %refs_0_.1, bf16[192,4096]{1,0:T(8,128)(2,1)} %refs_1_.1, bf16[192,4096]{1,0:T(8,128)(2,1)} %refs_2_.1, f32[64,192]{1,0:T(8,128)} %bitcast.6, f32[16,2,4096]{2,1,0:T(2,128)} %refs_4_.1, ...), custom_call_target="tpu_custom_call" | custom-call | tf_op jit(solution)/shard_map/everything/pallas_call | solution.py:835
  151.6 2.0 %deliver.1 = (f32[64,192]{1,0:T(8,128)}, bf16[2,16,24,384]{3,2,1,0:T(8,128)(2,1)}, f32[2,768]{1,0:T(2,128)}, f32[2]{0:T(128)}) custom-call(f32[64,192]{1,0:T(8,128)} %get-tuple-element.12.refs_0_, bf16[2,16,24,384]{3,2,1,0:T(8,128)(2,1)} %get-tuple-element.13.refs_1_, f32[2,768]{1,0:T(2,128)} %get-tuple-element.14.refs_2_, f32[2]{0:T(128)} %get-tuple-element.15.refs_3_), custom_call_target="tpu_custom_call" | custom-call | tf_op jit(solution)/shard_map/deliver/pallas_call | solution.py:886

commit v3 on v2

--- a/solution.py
+++ b/solution.py
@@ -49,7 +49,6 @@
     k_buf,
     v_buf,
     q_buf,
-    att_buf,
     part_buf,
     own_buf,
     mirror_buf,
@@ -262,7 +261,7 @@
             v_buf[h].reshape(n * rows, 2 * HD),
             preferred_element_type=jnp.float32,
         )
-        att_buf[src, :, h * HD : (h + 1) * HD] = (mixed[:, :HD] / mixed[:, HD:]).astype(jnp.bfloat16)
+        q_buf[src, :, h * HD : (h + 1) * HD] = (mixed[:, :HD] / mixed[:, HD:]).astype(jnp.bfloat16)
 
     def in_turn(first, heads, waits, done):
         count = half * len(heads)
@@ -306,7 +305,7 @@
     def project(x, src):
         packed = None
         for f in range(frames_dev):
-            rows_a = att_buf[src, f * per_frame : (f + 1) * per_frame, :]
+            rows_a = q_buf[src, f * per_frame : (f + 1) * per_frame, :]
             both = lax.dot_general(
                 rows_a, gain_buf[src * frames_dev + f], turned, preferred_element_type=jnp.float32
             )
@@ -557,9 +556,9 @@
     token = lax.broadcasted_iota(jnp.int32, (per_frame, ch), 0)
     row_id, col_id = token // GRID_W, lax.rem(token, GRID_W)
 
-    def one_frame(f, carry):
+    def one_frame(f):
         live = (me * frames_dev - 2 + f) >= 0
-        span = pl.ds(pl.multiple_of(f * per_frame, per_frame), per_frame)
+        span = slice(f * per_frame, (f + 1) * per_frame)
         for sub_a in range(2):
             for sub_b in range(2):
                 first_f = first_buf[2 * sub_a + sub_b, span, :].astype(f32)
@@ -585,9 +584,6 @@
                                 if source_a == (sub_a, di) and source_b == (sub_b, dj):
                                     tap = q * 3 + r
                                     window[f, 2 * a + b, :, tap * ch : (tap + 1) * ch] = shifted
-        return carry
-
-    lax.fori_loop(0, held, one_frame, 0)
 
     taps_n = 9
     conv_bias = conv_bias_ref[...][None, :]
@@ -596,13 +592,40 @@
             own = first_buf[ab, (f + 2) * per_frame : (f + 3) * per_frame, :].astype(f32)
             acc[(f * 4 + ab) * per_frame : (f * 4 + ab + 1) * per_frame, :] = own + conv_bias
 
-    def one_lag(lag, carry):
-        rows = window[pl.ds(lag, frames_dev)].reshape(frames_dev * 4 * per_frame, taps_n * ch)
-        weight = conv_w[pl.ds(lag * taps_n, taps_n)].reshape(taps_n * ch, ch)
-        acc[...] += jnp.dot(rows, weight, preferred_element_type=f32)
-        return carry
-
-    lax.fori_loop(0, 3, one_lag, 0)
+    frame_rows = 4 * per_frame
+    side_at = ch // 256 * 256
+
+    def one_lag(lag):
+        rows = window[lag : lag + frames_dev].reshape(frames_dev * frame_rows, taps_n * ch)
+        weight = conv_w[lag * taps_n : (lag + 1) * taps_n, :, :side_at].reshape(taps_n * ch, side_at)
+        acc[:, :side_at] += jnp.dot(rows, weight, preferred_element_type=f32)
+
+    def one_side(f):
+        rows = window[f].reshape(frame_rows, taps_n * ch)
+        lags = [lag for lag in range(3) if 0 <= f - lag < frames_dev]
+        while lags:
+            now, lags = lags[:2], lags[2:]
+            weight = jnp.concatenate(
+                [
+                    conv_w[lag * taps_n : (lag + 1) * taps_n, :, side_at:].reshape(taps_n * ch, ch - side_at)
+                    for lag in now
+                ],
+                axis=1,
+            )
+            both = jnp.dot(rows, weight, preferred_element_type=f32)
+            for i, lag in enumerate(now):
+                to = slice((f - lag) * frame_rows, (f - lag + 1) * frame_rows)
+                acc[to, side_at:] += both[:, i * (ch - side_at) : (i + 1) * (ch - side_at)]
+
+    for f in range(frames_dev):
+        one_frame(f)
+    for lag in range(3):
+        if lag + frames_dev < held:
+            one_frame(lag + frames_dev)
+        one_lag(lag)
+        one_side(lag)
+    for f in range(3, held):
+        one_side(f)
 
     for f in range(frames_dev):
         for a in range(2):
@@ -685,7 +708,7 @@
     yield
 
 
-MIX_IN, DECODE_IN, MIX_SCRATCH, HALO_AT = 10, 10, 36, 17
+MIX_IN, DECODE_IN, MIX_SCRATCH, HALO_AT = 10, 10, 35, 16
 SMALL_MIX, SMALL_DECODE = (3, 5, 6, 9), (1, 2, 4, 6, 7, 9)
 
 
@@ -764,7 +787,6 @@
     mix_scratch = [
         vmem((heads_here, n, rows, HD), b16),
         vmem((heads_here, n, rows, 2 * HD), b16),
-        vmem((n, rows, wide), b16),
         vmem((n, rows, wide), b16),
         vmem((n,) + part, b16),
         vmem((half,) + part, b16),

time: 154 us -> 153 us (level)
  no operation moved by 1% of the time
where the time goes in v3:
time: 153 us
  Pallas kernels  152 us (99%)
    pallas_call x1, Pallas kernels, everything(): pl.pallas_call(functools.partial(whole_kernel, n, heads_here), out_shape=...  150 us

profile of v3, /device:TPU:0, one launch (start us, length us, event | category | flops | bytes accessed | tf_op | source)
XLA Modules:
  0.0 153.1 jit_solution(3959756896970054608)
XLA Ops:
  0.6 150.4 %everything.1 = (f32[64,192]{1,0:T(8,128)}, bf16[2,16,24,384]{3,2,1,0:T(8,128)(2,1)}, f32[2,768]{1,0:T(2,128)}, f32[2]{0:T(128)}) custom-call(bf16[192,4096]{1,0:T(8,128)(2,1)} %refs_0_.1, bf16[192,4096]{1,0:T(8,128)(2,1)} %refs_1_.1, bf16[192,4096]{1,0:T(8,128)(2,1)} %refs_2_.1, f32[64,192]{1,0:T(8,128)} %bitcast.6, f32[16,2,4096]{2,1,0:T(2,128)} %refs_4_.1, ...), custom_call_target="tpu_custom_call" | custom-call | tf_op jit(solution)/shard_map/everything/pallas_call | solution.py:857
  151.0 2.0 %deliver.1 = (f32[64,192]{1,0:T(8,128)}, bf16[2,16,24,384]{3,2,1,0:T(8,128)(2,1)}, f32[2,768]{1,0:T(2,128)}, f32[2]{0:T(128)}) custom-call(f32[64,192]{1,0:T(8,128)} %get-tuple-element.12.refs_0_, bf16[2,16,24,384]{3,2,1,0:T(8,128)(2,1)} %get-tuple-element.13.refs_1_, f32[2,768]{1,0:T(2,128)} %get-tuple-element.14.refs_2_, f32[2]{0:T(128)} %get-tuple-element.15.refs_3_), custom_call_target="tpu_custom_call" | custom-call | tf_op jit(solution)/shard_map/deliver/pallas_call | solution.py:908

commit v4 on v3

--- a/solution.py
+++ b/solution.py
@@ -163,7 +163,6 @@
     for cp in locals_:
         cp.wait()
 
-    follow(0)
     lanes = table_buf.shape[2]
 
     def table_part(i, carry):
@@ -320,8 +319,7 @@
         part_buf[x, per_frame:, :] = sum_rows[x % 2].astype(jnp.bfloat16)
 
     for h in range(heads_here):
-        if h > 0:
-            follow(2 * h)
+        follow(2 * h)
         if h + 1 < heads_here:
             send_some(phases[2 * h + 2], 1, half)
             send_some(phases[2 * h + 3], 1, half)

time: 153 us -> 152 us (level)
  no operation moved by 1% of the time
where the time goes in v4:
time: 152 us
  Pallas kernels  151 us (99%)
    pallas_call x1, Pallas kernels, everything(): pl.pallas_call(functools.partial(whole_kernel, n, heads_here), out_shape=...  150 us

profile of v4, /device:TPU:0, one launch (start us, length us, event | category | flops | bytes accessed | tf_op | source)
XLA Modules:
  0.0 152.3 jit_solution(17398536375982757741)
XLA Ops:
  0.6 149.5 %everything.1 = (f32[64,192]{1,0:T(8,128)}, bf16[2,16,24,384]{3,2,1,0:T(8,128)(2,1)}, f32[2,768]{1,0:T(2,128)}, f32[2]{0:T(128)}) custom-call(bf16[192,4096]{1,0:T(8,128)(2,1)} %refs_0_.1, bf16[192,4096]{1,0:T(8,128)(2,1)} %refs_1_.1, bf16[192,4096]{1,0:T(8,128)(2,1)} %refs_2_.1, f32[64,192]{1,0:T(8,128)} %bitcast.6, f32[16,2,4096]{2,1,0:T(2,128)} %refs_4_.1, ...), custom_call_target="tpu_custom_call" | custom-call | tf_op jit(solution)/shard_map/everything/pallas_call | solution.py:855
  150.2 2.0 %deliver.1 = (f32[64,192]{1,0:T(8,128)}, bf16[2,16,24,384]{3,2,1,0:T(8,128)(2,1)}, f32[2,768]{1,0:T(2,128)}, f32[2]{0:T(128)}) custom-call(f32[64,192]{1,0:T(8,128)} %get-tuple-element.12.refs_0_, bf16[2,16,24,384]{3,2,1,0:T(8,128)(2,1)} %get-tuple-element.13.refs_1_, f32[2,768]{1,0:T(2,128)} %get-tuple-element.14.refs_2_, f32[2]{0:T(128)} %get-tuple-element.15.refs_3_), custom_call_target="tpu_custom_call" | custom-call | tf_op jit(solution)/shard_map/deliver/pallas_call | solution.py:906
